TPU v7x, 32 devices: a whole 2x2x4 slice. The times are simulated.
32 devices in a mesh: bx: 8 (over z, x), by: 4 (over y, core).
Axes of the slice: x: 2, y: 2, z: 4, core: 2. Of those that a mesh axis runs over, the one named last changes fastest.
Arguments:
- tokens: bfloat16 [8, 4, 1024, 512], P('bx', 'by'), may hold values from -6 to 6
- norm_gain: float32 [512], replicated, may hold values from 0.1 to 1.9
- w_query_key: bfloat16 [512, 1024], replicated
- w_value: bfloat16 [512, 512], replicated, may hold values from -1 to 1
- w_out: bfloat16 [512, 512], replicated, may hold values from -0.25 to 0.25
- cotangent: bfloat16 [8, 4, 1024, 512], P('bx', 'by'), may hold values from -6 to 6
- block_order: int32 [8, 4, 1024], P('bx', 'by'), may hold values from 0 to 1023, each once within a row
- neighbour_ids: int32 [8, 4, 4, 4], replicated, may hold values from 0 to 127, as said below
- neighbour_count: int32 [8, 4, 4], replicated, may hold values from 1 to 4
Outputs:
- branch_out: bfloat16 [8, 4, 1024, 512], P('bx', 'by')
- grad_tokens: float32 [8, 4, 1024, 512], P('bx', 'by')
- grad_w_query_key: float32 [512, 1024], replicated
- grad_w_value: float32 [512, 512], replicated
- grad_w_out: float32 [512, 512], replicated
- grad_norm_gain: float32 [512], replicated
Inputs may be any that keep to these rules, and one draw needn't show every extreme that they name: `neighbour_ids`: block ids are (x * 4 + y) * 4 + b. Entry j < neighbour_count of query block b on brick (x, y) names a block other than b itself, either another block of brick (x, y) or a block of a brick one step away along exactly one axis (x - 1, x + 1, y - 1 or y + 1); the live entries of one list differ. Entries from neighbour_count on hold the query block's own id. Over all query blocks of one brick, at most 2 distinct blocks of any one other brick are named, and every brick names exactly 2 blocks of some other brick. `block_order`: on every brick, a permutation of the arrival rows.
All inputs are finite; a program needn't handle non-finite values.
Results may differ from a plain program's by a relative error of at most 0.006.
The roundings to bfloat16 on the way count: a program that leaves them out, or rounds other values in their place, can miss the bound.
Values may be sent and summed in bfloat16 or wider, within the bound.
A program may use at most 256 MiB of HBM per device.

v0:
```python
import math
import jax
import jax.numpy as jnp
from jax import lax
from jax.sharding import PartitionSpec as P

HEADS = 8
BLK = 256
CAP = 2
EPSILON = 1e-06


def from_behind(block, axis, distance):
    devices = range(lax.axis_size(axis))
    route = [(i - distance, i) for i in devices if i - distance in devices]
    return lax.ppermute(block, axis, route)


def rms_rows(token_rows, gain_row):
    values = token_rows.astype(jnp.float32)
    inv_rms = lax.rsqrt(jnp.mean(values * values, axis=-1, keepdims=True) + EPSILON)
    return (values, inv_rms, (values * inv_rms * gain_row).astype(jnp.bfloat16))


def attend_block(query_rows, key_value_rows, live_cols, grad_context):
    features = query_rows.shape[-1]
    head_size = features // HEADS
    row_count = query_rows.shape[0]
    factor = 1.0 / math.sqrt(head_size)
    queries = query_rows.reshape(row_count, HEADS, head_size)
    kv_rows = key_value_rows.reshape(-1, 2 * features)
    key_rows = kv_rows[:, :features].reshape(-1, HEADS, head_size)
    value_rows = kv_rows[:, features:].reshape(-1, HEADS, head_size)
    grad_rows = grad_context.reshape(row_count, HEADS, head_size)
    scores = (
        jnp.einsum("ihd,jhd->hij", queries, key_rows, preferred_element_type=jnp.float32) * factor
    )
    scores = jnp.where(live_cols[None, None, :], scores, -1e30)
    row_max = jnp.max(scores, axis=-1, keepdims=True)
    powers = jnp.exp(scores - row_max)
    attn_probs = powers / jnp.sum(powers, axis=-1, keepdims=True)
    probs_low = attn_probs.astype(jnp.bfloat16)
    context = jnp.einsum(
        "hij,jhd->ihd", probs_low, value_rows, preferred_element_type=jnp.float32
    ).astype(jnp.bfloat16)
    grad_probs = jnp.einsum(
        "ihd,jhd->hij", grad_rows, value_rows, preferred_element_type=jnp.float32
    )
    centre = jnp.sum(attn_probs * grad_probs, axis=-1, keepdims=True)
    grad_scores = (attn_probs * (grad_probs - centre) * factor).astype(jnp.bfloat16)
    grad_query = jnp.einsum(
        "hij,jhd->ihd", grad_scores, key_rows, preferred_element_type=jnp.float32
    ).astype(jnp.bfloat16)
    grad_keys = jnp.einsum("hij,ihd->jhd", grad_scores, queries, preferred_element_type=jnp.float32)
    grad_values = jnp.einsum(
        "hij,ihd->jhd", probs_low, grad_rows, preferred_element_type=jnp.float32
    )
    slots = key_value_rows.shape[0]
    return (
        context.reshape(row_count, features),
        grad_query.reshape(row_count, features),
        grad_keys.reshape(slots, row_count, features),
        grad_values.reshape(slots, row_count, features),
    )


def shards(
    tokens,
    norm_gain,
    w_query_key,
    w_value,
    w_out,
    cotangent,
    block_order,
    neighbour_ids,
    neighbour_count,
):
    row_count = tokens.shape[2]
    features = tokens.shape[3]
    blocks = row_count // BLK
    slot_count = neighbour_ids.shape[3]
    extent_x = lax.axis_size("bx")
    extent_y = lax.axis_size("by")
    brick_x = lax.axis_index("bx")
    brick_y = lax.axis_index("by")
    my_brick = brick_x * extent_y + brick_y
    row_order = block_order[0, 0]
    sorted_rows = tokens[0, 0][row_order]
    sorted_grad = cotangent[0, 0][row_order]
    values, inv_rms, normed = rms_rows(sorted_rows, norm_gain)
    query_rows = jnp.dot(
        normed, w_query_key[:, :features], preferred_element_type=jnp.float32
    ).astype(jnp.bfloat16)
    w_pair = jnp.concatenate([w_query_key[:, features:], w_value], axis=1)
    key_value = jnp.dot(normed, w_pair, preferred_element_type=jnp.float32).astype(jnp.bfloat16)
    key_value = key_value.reshape(blocks, BLK, 2 * features)
    d_context = lax.dot_general(
        sorted_grad, w_out, (((1,), (1,)), ((), ())), preferred_element_type=jnp.float32
    ).astype(jnp.bfloat16)
    slot_range = jnp.arange(slot_count, dtype=jnp.int32)
    block_range = jnp.arange(blocks, dtype=jnp.int32)
    side_range = jnp.arange(1, 5, dtype=jnp.int32)
    my_ids = neighbour_ids[brick_x, brick_y]
    my_count = neighbour_count[brick_x, brick_y]
    live_slots = slot_range[None, :] < my_count[:, None]
    owner_brick = my_ids // blocks
    offset = my_ids % blocks
    delta_x = owner_brick // extent_y - brick_x
    delta_y = owner_brick % extent_y - brick_y
    segment = jnp.where(
        delta_x == -1,
        1,
        jnp.where(delta_x == 1, 2, jnp.where(delta_y == -1, 3, jnp.where(delta_y == 1, 4, 0))),
    )

    def selection_for(req_x, req_y):
        safe_x = jnp.clip(req_x, 0, extent_x - 1)
        safe_y = jnp.clip(req_y, 0, extent_y - 1)
        req_ids = neighbour_ids[safe_x, safe_y]
        req_count = neighbour_count[safe_x, safe_y]
        req_live = slot_range[None, :] < req_count[:, None]
        from_me = req_live & (req_ids // blocks == my_brick)
        wanted = jnp.any(
            from_me[:, :, None] & ((req_ids % blocks)[:, :, None] == block_range), axis=(0, 1)
        )
        ranks = jnp.cumsum(wanted.astype(jnp.int32)) - 1
        pick_rows = wanted[None, :] & (ranks[None, :] == jnp.arange(CAP, dtype=jnp.int32)[:, None])
        return pick_rows.astype(jnp.bfloat16)

    choosers = {}
    for shift_step in (1, -1):
        choosers["bx", shift_step] = selection_for(brick_x + shift_step, brick_y)
        choosers["by", shift_step] = selection_for(brick_x, brick_y + shift_step)
    side_match = (segment[:, :, None, None] == side_range[None, None, :, None]) & (
        offset[:, :, None, None] == block_range[None, None, None, :]
    )
    wanted_here = jnp.any(live_slots[:, :, None, None] & side_match, axis=(0, 1))
    side_ranks = jnp.cumsum(wanted_here.astype(jnp.int32), axis=1) - 1
    rank_of = jnp.sum(jnp.where(side_match, side_ranks[None, None, :, :], 0), axis=(2, 3))
    entry_index = jnp.where(segment == 0, offset, blocks + (segment - 1) * CAP + rank_of)

    def outgoing(source, side_key):
        picked = jnp.einsum(
            "co,otf->ctf", choosers[side_key], source, preferred_element_type=jnp.float32
        )
        return picked.astype(jnp.bfloat16)

    def incoming(returned, side_key):
        return jnp.einsum(
            "co,ctf->otf", choosers[side_key], returned, preferred_element_type=jnp.float32
        )

    fetched = {}
    for shift_step in (1, -1):
        fetched["bx", shift_step] = from_behind(
            outgoing(key_value, ("bx", shift_step)), "bx", shift_step
        )
    for shift_step in (1, -1):
        fetched["by", shift_step] = from_behind(
            outgoing(key_value, ("by", shift_step)), "by", shift_step
        )
    key_pool = jnp.concatenate(
        [key_value, fetched["bx", 1], fetched["bx", -1], fetched["by", 1], fetched["by", -1]],
        axis=0,
    )
    key_index = jnp.concatenate([block_range[:, None], entry_index], axis=1)
    live_keys = jnp.concatenate([jnp.ones((blocks, 1), dtype=jnp.bool_), live_slots], axis=1)
    pool_rows = key_pool.shape[0]

    def per_block(totals, block_item):
        block_query, block_grad, key_ids, live_here = block_item
        live_cols = jnp.repeat(live_here, BLK)
        context, grad_query, key_terms, value_terms = attend_block(
            block_query, key_pool[key_ids], live_cols, block_grad
        )
        key_total = totals[0].at[key_ids].add(key_terms)
        value_total = totals[1].at[key_ids].add(value_terms)
        return ((key_total, value_total), (context, grad_query))

    empty_total = jnp.zeros((pool_rows, BLK, features), jnp.float32)
    (key_total, value_total), (context, grad_query) = lax.scan(
        per_block,
        (empty_total, empty_total),
        (
            query_rows.reshape(blocks, BLK, features),
            d_context.reshape(blocks, BLK, features),
            key_index,
            live_keys,
        ),
    )
    seg_rows = (pool_rows - blocks) // 4

    def segment_rows(index):
        lower = blocks + index * seg_rows
        upper = lower + seg_rows
        return jnp.concatenate([key_total[lower:upper], value_total[lower:upper]], axis=-1).astype(
            jnp.bfloat16
        )

    own_grad = jnp.concatenate([key_total[:blocks], value_total[:blocks]], axis=-1)
    for shift_step, index in ((1, 0), (-1, 1)):
        returned = from_behind(segment_rows(index), "bx", -shift_step)
        own_grad = own_grad + incoming(returned, ("bx", shift_step))
    for shift_step, index in ((1, 2), (-1, 3)):
        returned = from_behind(segment_rows(index), "by", -shift_step)
        own_grad = own_grad + incoming(returned, ("by", shift_step))
    grad_kv = own_grad.astype(jnp.bfloat16).reshape(row_count, 2 * features)
    context = context.reshape(row_count, features)
    grad_query = grad_query.reshape(row_count, features)
    out_rows = jnp.dot(context, w_out, preferred_element_type=jnp.float32).astype(jnp.bfloat16)
    grad_out_part = lax.dot_general(
        context, sorted_grad, (((0,), (0,)), ((), ())), preferred_element_type=jnp.float32
    )
    grad_proj = jnp.concatenate([grad_query, grad_kv], axis=1)
    w_all = jnp.concatenate([w_query_key, w_value], axis=1)
    grad_normed = lax.dot_general(
        grad_proj, w_all, (((1,), (1,)), ((), ())), preferred_element_type=jnp.float32
    )
    grad_all_part = lax.dot_general(
        normed, grad_proj, (((0,), (0,)), ((), ())), preferred_element_type=jnp.float32
    )
    gain_part = jnp.sum(grad_normed * (values * inv_rms), axis=0)
    scaled_grad = grad_normed * norm_gain
    grad_rows = inv_rms * scaled_grad - values * (inv_rms * inv_rms * inv_rms) * jnp.mean(
        values * scaled_grad, axis=-1, keepdims=True
    )
    grad_qk, grad_val, grad_output, grad_gain = lax.psum(
        (
            grad_all_part[:, : 2 * features],
            grad_all_part[:, 2 * features :],
            grad_out_part,
            gain_part,
        ),
        ("bx", "by"),
    )
    inverse = (
        jnp.zeros((row_count,), jnp.int32).at[row_order].set(jnp.arange(row_count, dtype=jnp.int32))
    )
    branch_out = out_rows[inverse][None, None]
    grad_tokens = grad_rows[inverse][None, None]
    return (branch_out, grad_tokens, grad_qk, grad_val, grad_output, grad_gain)


def solution(mesh):
    placed = (
        P("bx", "by", None, None),
        P(),
        P(),
        P(),
        P(),
        P("bx", "by", None, None),
        P("bx", "by", None),
        P(),
        P(),
    )
    return jax.shard_map(
        shards,
        mesh=mesh,
        in_specs=placed,
        out_specs=(P("bx", "by", None, None), P("bx", "by", None, None), P(), P(), P(), P()),
        check_vma=False,
    )
```

profile of v0, /device:TPU:0, one launch (start us, length us, event | category | flops | bytes accessed | tf_op | source)
XLA Modules:
  0.0 818.0 jit_solution(14798237451019191101)
XLA Ops:
  57.7 15.0 %collective-permute-done = bf16[2,256,1024]{2,0,1:T(2,128)(2,1)} collective-permute-done((bf16[2,256,1024]{2,0,1:T(2,128)(2,1)}, bf16[2,256,1024]{2,0,1:T(2,128)(2,1)}, u32[]{:S(2)}, u32[]{:S(2)}) %collective-permute-start) | collective-permute-done | bytes 1048608 | tf_op jit(solution)/shard_map/ppermute | solution.py:16
  86.7 490.7 %while.16 = (s32[]{:T(128)}, f32[12,256,512]{2,1,0:T(8,128)}, f32[12,256,512]{2,1,0:T(8,128)}, bf16[4,256,512]{2,1,0:T(8,128)(2,1)}, bf16[4,256,512]{2,1,0:T(8,1...) while((s32[]{:T(128)}, f32[12,256,512]{2,1,0:T(8,128)}, ...), condition=%wide.region_18.19_spmd, body=%wide.region_12.18_spmd.sunk | while | flops 2759343360 | bytes 145281360 | solution.py:181
  98.4 8.4 %fusion.202 = (f32[8,256]{1,0:T(8,128)S(1)}, f32[8,256,1280]{2,1,0:T(8,128)}) fusion(pred[1280]{0:T(1024)(128)(4,1)S(1)} %broadcast_in_dim.159, bf16[256,8,64]{0,2,1:T(8,128)(2,1)S(1)} %bitcast.165, bf16[1280,8,64]{0,2,1:T(8,128)(2,1)} %bitcast.159), kind=kOutput, calls=%fused_computation.249.clone.1 | convolution fusion | flops 346031360 | bytes 12068096 | tf_op jit(solution)/shard_map/while/body/eval_jaxpr/sub | solution.py:40
  116.2 19.1 %fusion.204 = bf16[8,64,256]{2,1,0:T(8,128)(2,1)S(1)} fusion(bf16[1280,8,64]{0,2,1:T(8,128)(2,1)} %bitcast.160, f32[8,256,1280]{2,1,0:T(8,128)} %fusion.201, f32[8,256,1280]{2,1,0:T(8,128)} %get-tuple-element.228, f32[8,256]{1,0:T(8,128)S(1)} %get-tuple-element.229), kind=kOutput, calls=%fused_computation.29.clone.1 | convolution fusion | flops 354028800 | bytes 22552576 | tf_op jit(solution)/shard_map/while/body/eval_jaxpr/hij,jhd->ihd/dot_general | solution.py:51
  141.4 25.7 %fusion.203 = f32[1280,8,64]{0,2,1:T(8,128)} fusion(bf16[256,8,64]{0,2,1:T(8,128)(2,1)S(1)} %bitcast.167, f32[8,256,1280]{2,1,0:T(8,128)} %fusion.201, f32[8,256,1280]{2,1,0:T(8,128)} %get-tuple-element.228, f32[8,256]{1,0:T(8,128)S(1)} %get-tuple-element.229), kind=kOutput, calls=%fused_computation.23.clone.1 | convolution fusion | flops 353897728 | bytes 23863296 | tf_op jit(solution)/shard_map/while/body/eval_jaxpr/hij,ihd->jhd/dot_general | solution.py:54
  176.4 8.5 %scatter_fusion = f32[12,256,512]{2,1,0:T(8,128)} fusion(f32[12,256,512]{2,1,0:T(8,128)} %get-tuple-element.244, s32[5]{0:T(128)S(1)} %fusion.199, f32[5,256,512]{2,1,0:T(8,128)} %copy.111), kind=kCustom, calls=%fused_computation.5.clone.1 | custom fusion | flops 655360 | bytes 7864340 | tf_op jit(solution)/shard_map/while/body/eval_jaxpr/scatter-add | solution.py:176
  199.2 8.4 %scatter_fusion.1 = f32[12,256,512]{2,1,0:T(8,128)} fusion(f32[12,256,512]{2,1,0:T(8,128)} %get-tuple-element.245, s32[5]{0:T(128)S(1)} %fusion.199, f32[5,256,512]{2,1,0:T(8,128)} %copy.112), kind=kCustom, calls=%fused_computation.6.clone.1 | custom fusion | flops 655360 | bytes 7864340 | tf_op jit(solution)/shard_map/while/body/eval_jaxpr/scatter-add | solution.py:177
  219.3 8.4 %fusion.202 = (f32[8,256]{1,0:T(8,128)S(1)}, f32[8,256,1280]{2,1,0:T(8,128)}) fusion(pred[1280]{0:T(1024)(128)(4,1)S(1)} %broadcast_in_dim.159, bf16[256,8,64]{0,2,1:T(8,128)(2,1)S(1)} %bitcast.165, bf16[1280,8,64]{0,2,1:T(8,128)(2,1)} %bitcast.159), kind=kOutput, calls=%fused_computation.249.clone.1 | convolution fusion | flops 346031360 | bytes 12068096 | tf_op jit(solution)/shard_map/while/body/eval_jaxpr/sub | solution.py:40
  237.2 19.1 %fusion.204 = bf16[8,64,256]{2,1,0:T(8,128)(2,1)S(1)} fusion(bf16[1280,8,64]{0,2,1:T(8,128)(2,1)} %bitcast.160, f32[8,256,1280]{2,1,0:T(8,128)} %fusion.201, f32[8,256,1280]{2,1,0:T(8,128)} %get-tuple-element.228, f32[8,256]{1,0:T(8,128)S(1)} %get-tuple-element.229), kind=kOutput, calls=%fused_computation.29.clone.1 | convolution fusion | flops 354028800 | bytes 22552576 | tf_op jit(solution)/shard_map/while/body/eval_jaxpr/hij,jhd->ihd/dot_general | solution.py:51
  262.3 25.7 %fusion.203 = f32[1280,8,64]{0,2,1:T(8,128)} fusion(bf16[256,8,64]{0,2,1:T(8,128)(2,1)S(1)} %bitcast.167, f32[8,256,1280]{2,1,0:T(8,128)} %fusion.201, f32[8,256,1280]{2,1,0:T(8,128)} %get-tuple-element.228, f32[8,256]{1,0:T(8,128)S(1)} %get-tuple-element.229), kind=kOutput, calls=%fused_computation.23.clone.1 | convolution fusion | flops 353897728 | bytes 23863296 | tf_op jit(solution)/shard_map/while/body/eval_jaxpr/hij,ihd->jhd/dot_general | solution.py:54
  297.3 8.4 %scatter_fusion = f32[12,256,512]{2,1,0:T(8,128)} fusion(f32[12,256,512]{2,1,0:T(8,128)} %get-tuple-element.244, s32[5]{0:T(128)S(1)} %fusion.199, f32[5,256,512]{2,1,0:T(8,128)} %copy.111), kind=kCustom, calls=%fused_computation.5.clone.1 | custom fusion | flops 655360 | bytes 7864340 | tf_op jit(solution)/shard_map/while/body/eval_jaxpr/scatter-add | solution.py:176
  320.1 8.4 %scatter_fusion.1 = f32[12,256,512]{2,1,0:T(8,128)} fusion(f32[12,256,512]{2,1,0:T(8,128)} %get-tuple-element.245, s32[5]{0:T(128)S(1)} %fusion.199, f32[5,256,512]{2,1,0:T(8,128)} %copy.112), kind=kCustom, calls=%fused_computation.6.clone.1 | custom fusion | flops 655360 | bytes 7864340 | tf_op jit(solution)/shard_map/while/body/eval_jaxpr/scatter-add | solution.py:177
  340.2 8.4 %fusion.202 = (f32[8,256]{1,0:T(8,128)S(1)}, f32[8,256,1280]{2,1,0:T(8,128)}) fusion(pred[1280]{0:T(1024)(128)(4,1)S(1)} %broadcast_in_dim.159, bf16[256,8,64]{0,2,1:T(8,128)(2,1)S(1)} %bitcast.165, bf16[1280,8,64]{0,2,1:T(8,128)(2,1)} %bitcast.159), kind=kOutput, calls=%fused_computation.249.clone.1 | convolution fusion | flops 346031360 | bytes 12068096 | tf_op jit(solution)/shard_map/while/body/eval_jaxpr/sub | solution.py:40
  358.0 19.1 %fusion.204 = bf16[8,64,256]{2,1,0:T(8,128)(2,1)S(1)} fusion(bf16[1280,8,64]{0,2,1:T(8,128)(2,1)} %bitcast.160, f32[8,256,1280]{2,1,0:T(8,128)} %fusion.201, f32[8,256,1280]{2,1,0:T(8,128)} %get-tuple-element.228, f32[8,256]{1,0:T(8,128)S(1)} %get-tuple-element.229), kind=kOutput, calls=%fused_computation.29.clone.1 | convolution fusion | flops 354028800 | bytes 22552576 | tf_op jit(solution)/shard_map/while/body/eval_jaxpr/hij,jhd->ihd/dot_general | solution.py:51
  383.1 25.7 %fusion.203 = f32[1280,8,64]{0,2,1:T(8,128)} fusion(bf16[256,8,64]{0,2,1:T(8,128)(2,1)S(1)} %bitcast.167, f32[8,256,1280]{2,1,0:T(8,128)} %fusion.201, f32[8,256,1280]{2,1,0:T(8,128)} %get-tuple-element.228, f32[8,256]{1,0:T(8,128)S(1)} %get-tuple-element.229), kind=kOutput, calls=%fused_computation.23.clone.1 | convolution fusion | flops 353897728 | bytes 23863296 | tf_op jit(solution)/shard_map/while/body/eval_jaxpr/hij,ihd->jhd/dot_general | solution.py:54
  418.2 8.4 %scatter_fusion = f32[12,256,512]{2,1,0:T(8,128)} fusion(f32[12,256,512]{2,1,0:T(8,128)} %get-tuple-element.244, s32[5]{0:T(128)S(1)} %fusion.199, f32[5,256,512]{2,1,0:T(8,128)} %copy.111), kind=kCustom, calls=%fused_computation.5.clone.1 | custom fusion | flops 655360 | bytes 7864340 | tf_op jit(solution)/shard_map/while/body/eval_jaxpr/scatter-add | solution.py:176
  440.9 8.3 %scatter_fusion.1 = f32[12,256,512]{2,1,0:T(8,128)} fusion(f32[12,256,512]{2,1,0:T(8,128)} %get-tuple-element.245, s32[5]{0:T(128)S(1)} %fusion.199, f32[5,256,512]{2,1,0:T(8,128)} %copy.112), kind=kCustom, calls=%fused_computation.6.clone.1 | custom fusion | flops 655360 | bytes 7864340 | tf_op jit(solution)/shard_map/while/body/eval_jaxpr/scatter-add | solution.py:177
  461.0 8.4 %fusion.202 = (f32[8,256]{1,0:T(8,128)S(1)}, f32[8,256,1280]{2,1,0:T(8,128)}) fusion(pred[1280]{0:T(1024)(128)(4,1)S(1)} %broadcast_in_dim.159, bf16[256,8,64]{0,2,1:T(8,128)(2,1)S(1)} %bitcast.165, bf16[1280,8,64]{0,2,1:T(8,128)(2,1)} %bitcast.159), kind=kOutput, calls=%fused_computation.249.clone.1 | convolution fusion | flops 346031360 | bytes 12068096 | tf_op jit(solution)/shard_map/while/body/eval_jaxpr/sub | solution.py:40
  478.8 19.1 %fusion.204 = bf16[8,64,256]{2,1,0:T(8,128)(2,1)S(1)} fusion(bf16[1280,8,64]{0,2,1:T(8,128)(2,1)} %bitcast.160, f32[8,256,1280]{2,1,0:T(8,128)} %fusion.201, f32[8,256,1280]{2,1,0:T(8,128)} %get-tuple-element.228, f32[8,256]{1,0:T(8,128)S(1)} %get-tuple-element.229), kind=kOutput, calls=%fused_computation.29.clone.1 | convolution fusion | flops 354028800 | bytes 22552576 | tf_op jit(solution)/shard_map/while/body/eval_jaxpr/hij,jhd->ihd/dot_general | solution.py:51
  503.9 25.7 %fusion.203 = f32[1280,8,64]{0,2,1:T(8,128)} fusion(bf16[256,8,64]{0,2,1:T(8,128)(2,1)S(1)} %bitcast.167, f32[8,256,1280]{2,1,0:T(8,128)} %fusion.201, f32[8,256,1280]{2,1,0:T(8,128)} %get-tuple-element.228, f32[8,256]{1,0:T(8,128)S(1)} %get-tuple-element.229), kind=kOutput, calls=%fused_computation.23.clone.1 | convolution fusion | flops 353897728 | bytes 23863296 | tf_op jit(solution)/shard_map/while/body/eval_jaxpr/hij,ihd->jhd/dot_general | solution.py:54
  539.0 8.1 scatter_fusion
  626.8 15.0 %collective-permute-done.5 = bf16[2,256,1024]{2,0,1:T(2,128)(2,1)} collective-permute-done((bf16[2,256,1024]{2,0,1:T(2,128)(2,1)S(1)}, bf16[2,256,1024]{2,0,1:T(2,128)(2,1)}, u32[]{:S(2)}, u32[]{:S(2)}) %collective-permute-start.5) | collective-permute-done | bytes 1048608 | tf_op jit(solution)/shard_map/ppermute | solution.py:16
  678.9 43.6 %psum.31 = f32[512]{0:T(512)} all-reduce(f32[512]{0:T(512)S(1)} %get-tuple-element.95), channel_id=1, replica_groups=mesh['bx'=8,'by'=4] {'bx','by'}, use_global_device_ids=true, to_apply=%region_25.26 | all-reduce | flops 512 | bytes 4096 | tf_op jit(solution)/shard_map/psum | solution.py:227
  722.5 82.9 %all-reduce.4.cloned.1.call-done = (f32[512,1024]{1,0:T(8,128)}, f32[512,512]{1,0:T(8,128)}, f32[512,512]{1,0:T(8,128)}) async-done(((f32[512,1024]{1,0:T(8,128)}, f32[512,512]{1,0:T(8,128)}, f32[512,512]{1,0:T(8,128)}), (f32[512,1024]{1,0:T(8,128)}, f32[512,512]{1,0:T(8,128)}, f32[512,512]{1,0:T(8,128)})) %all-reduce.4.cloned.1.call-update) | async-done | bytes 4194320 | tf_op jit(solution)/shard_map/psum | solution.py:227
  (311 shorter events, 366.3 us)
Async XLA Ops:
  7.2 798.2 %all-reduce.4.cloned.1.call-start = ((), (), s32[]{:S(2)}) async-start(), calls=%async_computation | async-start | bytes 8388608 | tf_op jit(solution)/shard_map/psum | solution.py:227
  15.4 38.5 %copy-start.6 = (bf16[1024,512]{1,0:T(8,128)(2,1)}, bf16[1024,512]{1,0:T(8,128)(2,1)S(1)}, u32[]{:S(2)}) copy-start(bf16[1024,512]{1,0:T(8,128)(2,1)S(1)} %gather_fusion.1) | copy-start | bytes 3145732
  16.3 37.6 %copy-start.20 = (f32[1024]{0:T(1024)}, f32[1024]{0:T(1024)S(1)}, u32[]{:S(2)}) copy-start(f32[1024]{0:T(1024)S(1)} %get-tuple-element.145) | copy-start | bytes 12292
  22.6 50.0 %collective-permute-start = (bf16[2,256,1024]{2,0,1:T(2,128)(2,1)}, bf16[2,256,1024]{2,0,1:T(2,128)(2,1)}, u32[]{:S(2)}, u32[]{:S(2)}) collective-permute-start(bf16[2,256,1024]{2,0,1:T(2,128)(2,1)} %convolution_convert_fusion.4), channel_id=1, source_target_pairs={{0,4},{4,8},{8,12},{12,16},{16,20},{20,24},{24,28},{1,5},{5,9},{9,... | collective-permute-start | bytes 3145736 | tf_op jit(solution)/shard_map/ppermute | solution.py:16
  28.6 10.5 %copy-start.28 = (pred[4]{0:T(512)(128)(4,1)}, pred[4]{0:T(512)(128)(4,1)S(1)}, u32[]{:S(2)}) copy-start(pred[4]{0:T(512)(128)(4,1)S(1)} %fusion.67) | copy-start | bytes 16
  33.1 41.0 %collective-permute-start.1 = (bf16[2,256,1024]{2,0,1:T(2,128)(2,1)}, bf16[2,256,1024]{2,0,1:T(2,128)(2,1)}, u32[]{:S(2)}, u32[]{:S(2)}) collective-permute-start(bf16[2,256,1024]{2,0,1:T(2,128)(2,1)} %convolution_convert_fusion.3), channel_id=1, source_target_pairs={{4,0},{8,4},{12,8},{16,12},{20,16},{24,20},{28,24},{5,1},{9,5},{13... | collective-permute-start | bytes 3145736 | tf_op jit(solution)/shard_map/ppermute | solution.py:16
  34.6 11.6 %copy-start.30 = (pred[4]{0:T(512)(128)(4,1)}, pred[4]{0:T(512)(128)(4,1)S(1)}, u32[]{:S(2)}) copy-start(pred[4]{0:T(512)(128)(4,1)S(1)} %fusion.69) | copy-start | bytes 16
  34.8 11.4 %copy-start.38 = (s32[4]{0:T(128)}, s32[4]{0:T(128)S(1)}, u32[]{:S(2)}) copy-start(s32[4]{0:T(128)S(1)} %add_bitcast_fusion.1) | copy-start | bytes 52
  39.1 36.5 %collective-permute-start.2 = (bf16[2,256,1024]{2,0,1:T(2,128)(2,1)}, bf16[2,256,1024]{2,0,1:T(2,128)(2,1)}, u32[]{:S(2)}, u32[]{:S(2)}) collective-permute-start(bf16[2,256,1024]{2,0,1:T(2,128)(2,1)} %convolution_convert_fusion.2), channel_id=1, source_target_pairs={{0,1},{1,2},{2,3},{4,5},{5,6},{6,7},{8,9},{9,10},{10,11},{12,13},{... | collective-permute-start | bytes 3145736 | tf_op jit(solution)/shard_map/ppermute | solution.py:16
  46.2 30.9 %collective-permute-start.3 = (bf16[2,256,1024]{2,0,1:T(2,128)(2,1)}, bf16[2,256,1024]{2,0,1:T(2,128)(2,1)}, u32[]{:S(2)}, u32[]{:S(2)}) collective-permute-start(bf16[2,256,1024]{2,0,1:T(2,128)(2,1)} %convolution_convert_fusion.1), channel_id=1, source_target_pairs={{1,0},{2,1},{3,2},{5,4},{6,5},{7,6},{9,8},{10,9},{11,10},{13,12},{... | collective-permute-start | bytes 3145736 | tf_op jit(solution)/shard_map/ppermute | solution.py:16
  116.2 19.3 %copy-start.2 = (bf16[1280,512]{0,1:T(8,128)(2,1)S(1)}, bf16[1280,512]{0,1:T(8,128)(2,1)}, u32[]{:S(2)}) copy-start(bf16[1280,512]{0,1:T(8,128)(2,1)} %copy.109) | copy-start | bytes 3932164 | tf_op jit(solution)/shard_map/while
  237.2 19.3 %copy-start.2 = (bf16[1280,512]{0,1:T(8,128)(2,1)S(1)}, bf16[1280,512]{0,1:T(8,128)(2,1)}, u32[]{:S(2)}) copy-start(bf16[1280,512]{0,1:T(8,128)(2,1)} %copy.109) | copy-start | bytes 3932164 | tf_op jit(solution)/shard_map/while
  358.0 19.3 %copy-start.2 = (bf16[1280,512]{0,1:T(8,128)(2,1)S(1)}, bf16[1280,512]{0,1:T(8,128)(2,1)}, u32[]{:S(2)}) copy-start(bf16[1280,512]{0,1:T(8,128)(2,1)} %copy.109) | copy-start | bytes 3932164 | tf_op jit(solution)/shard_map/while
  478.8 19.3 %copy-start.2 = (bf16[1280,512]{0,1:T(8,128)(2,1)S(1)}, bf16[1280,512]{0,1:T(8,128)(2,1)}, u32[]{:S(2)}) copy-start(bf16[1280,512]{0,1:T(8,128)(2,1)} %copy.109) | copy-start | bytes 3932164 | tf_op jit(solution)/shard_map/while
  585.5 19.3 %slice-start = ((s8[6291456]{0:T(1024)(128)(4,1)}), s8[4194304]{0:T(1024)(128)(4,1)S(1)}, s32[]{:S(2)}) async-start(s8[6291456]{0:T(1024)(128)(4,1)} %bitcast.152), calls=%async_computation.1 | async-start | bytes 8388608
  588.9 15.9 %slice-start.1 = ((s8[6291456]{0:T(1024)(128)(4,1)}), s8[2097152]{0:T(1024)(128)(4,1)S(1)}, s32[]{:S(2)}) async-start(s8[6291456]{0:T(1024)(128)(4,1)} %bitcast.152), calls=%async_computation.2 | async-start | bytes 4194304
  592.6 31.4 %collective-permute-start.4 = (bf16[2,256,1024]{2,0,1:T(2,128)(2,1)}, bf16[2,256,1024]{2,0,1:T(2,128)(2,1)}, u32[]{:S(2)}, u32[]{:S(2)}) collective-permute-start(bf16[2,256,1024]{2,0,1:T(2,128)(2,1)} %pad_maximum_fusion.3), channel_id=1, source_target_pairs={{4,0},{8,4},{12,8},{16,12},{20,16},{24,20},{28,24},{5,1},{9,5},{13... | collective-permute-start | bytes 3145736 | tf_op jit(solution)/shard_map/ppermute | solution.py:16
  594.8 47.1 %collective-permute-start.5 = (bf16[2,256,1024]{2,0,1:T(2,128)(2,1)S(1)}, bf16[2,256,1024]{2,0,1:T(2,128)(2,1)}, u32[]{:S(2)}, u32[]{:S(2)}) collective-permute-start(bf16[2,256,1024]{2,0,1:T(2,128)(2,1)S(1)} %pad_maximum_fusion.4), channel_id=1, source_target_pairs={{0,4},{4,8},{8,12},{12,16},{16,20},{20,24},{24,28},{1,5},{5,9},{9,... | collective-permute-start | bytes 3145736 | tf_op jit(solution)/shard_map/ppermute | solution.py:16
  601.5 43.1 %collective-permute-start.6 = (bf16[2,256,1024]{2,0,1:T(2,128)(2,1)S(1)}, bf16[2,256,1024]{2,0,1:T(2,128)(2,1)}, u32[]{:S(2)}, u32[]{:S(2)}) collective-permute-start(bf16[2,256,1024]{2,0,1:T(2,128)(2,1)S(1)} %pad_maximum_fusion.5), channel_id=1, source_target_pairs={{1,0},{2,1},{3,2},{5,4},{6,5},{7,6},{9,8},{10,9},{11,10},{13,12},{... | collective-permute-start | bytes 3145736 | tf_op jit(solution)/shard_map/ppermute | solution.py:16
  615.5 32.0 %collective-permute-start.7 = (bf16[2,256,1024]{2,0,1:T(2,128)(2,1)}, bf16[2,256,1024]{2,0,1:T(2,128)(2,1)S(1)}, u32[]{:S(2)}, u32[]{:S(2)}) collective-permute-start(bf16[2,256,1024]{2,0,1:T(2,128)(2,1)} %pad_maximum_fusion.6), channel_id=1, source_target_pairs={{0,1},{1,2},{2,3},{4,5},{5,6},{6,7},{8,9},{9,10},{10,11},{12,13},{... | collective-permute-start | bytes 3145736 | tf_op jit(solution)/shard_map/ppermute | solution.py:16
  623.9 17.9 %copy-start.29 = (pred[4]{0:T(512)(128)(4,1)S(1)}, pred[4]{0:T(512)(128)(4,1)}, u32[]{:S(2)}) copy-start(pred[4]{0:T(512)(128)(4,1)} %copy-done.28) | copy-start | bytes 16
  623.9 17.9 %copy-start.37 = (s32[4]{0:T(128)S(1)}, s32[4]{0:T(128)}, u32[]{:S(2)}) copy-start(s32[4]{0:T(128)} %copy-done.36) | copy-start | bytes 52
  626.7 17.9 %copy-start.31 = (pred[4]{0:T(512)(128)(4,1)S(1)}, pred[4]{0:T(512)(128)(4,1)}, u32[]{:S(2)}) copy-start(pred[4]{0:T(512)(128)(4,1)} %copy-done.30) | copy-start | bytes 16
  626.8 17.9 %copy-start.39 = (s32[4]{0:T(128)S(1)}, s32[4]{0:T(128)}, u32[]{:S(2)}) copy-start(s32[4]{0:T(128)} %copy-done.38) | copy-start | bytes 52
  (40 other events, 180.0 us)
Sparse Core Ops, SparseCore 0:
  657.8 147.5 all-reduce.3
where the time goes:
time: 829 us; the launch traced here: 818 us
  matrix products  323 us (39%)
  local copies, waits for them, and re-layouts  215 us (26%)
  waiting for transfers between devices  113 us (14%)
  other arithmetic  76.7 us (9%)
  blocking collectives  43.6 us (5%)
  starting transfers between devices  23 us (3%)
  between operations  15.4 us (2%)
    dot_general x4, matrix products, attend_block(): jnp.einsum('hij,ihd->jhd', grad_scores, queries, preferred_element_type=j...  103 us
    psum x1, waiting for transfers between devices, shards(): lax.psum((grad_all_part[:, :2 * features], grad_all_part[:, 2 * features:...  82.9 us
    dot_general x4, matrix products, attend_block(): jnp.einsum('hij,jhd->ihd', grad_scores, key_rows, preferred_element_type=...  76.5 us
    psum x1, blocking collectives, shards(): lax.psum((grad_all_part[:, :2 * features], grad_all_part[:, 2 * features:...  43.6 us
    reshape x8, local copies, waits for them, and re-layouts, attend_block(): grad_keys.reshape(slots, row_count, features)  37.3 us
    reshape x8, local copies, waits for them, and re-layouts, attend_block(): grad_values.reshape(slots, row_count, features)  37.3 us
    sub x4, matrix products, attend_block(): powers = jnp.exp(scores - row_max)  33.7 us
    scatter-add x4, other arithmetic, per_block(): key_total = totals[0].at[key_ids].add(key_terms)  33.5 us
  transfers between devices with their start and end apart: 9, of which 3 were waited for; matrix products, arithmetic and copies ran while one was open for 9% of the time, Pallas kernels for 0%

commit v1 on v0

--- a/solution.py
+++ b/solution.py
@@ -225,13 +225,16 @@
         values * scaled_grad, axis=-1, keepdims=True
     )
     grad_qk, grad_val, grad_output, grad_gain = lax.psum(
-        (
-            grad_all_part[:, : 2 * features],
-            grad_all_part[:, 2 * features :],
-            grad_out_part,
-            gain_part,
+        lax.psum(
+            (
+                grad_all_part[:, : 2 * features],
+                grad_all_part[:, 2 * features :],
+                grad_out_part,
+                gain_part,
+            ),
+            "by",
         ),
-        ("bx", "by"),
+        "bx",
     )
     inverse = (
         jnp.zeros((row_count,), jnp.int32).at[row_order].set(jnp.arange(row_count, dtype=jnp.int32))

time: 829 us -> 932 us (1.12)
  waiting for transfers between devices: 113 us -> 230 us
  blocking collectives: 43.6 us -> 29.2 us
    psum x0 -> x1, waiting for transfers between devices: none -> 110 us  [shards(): lax.psum(lax.psum((grad_all_part[:, :2 * features], grad_all_part[:, 2 *...]
    psum x1, blocking collectives: 43.6 us -> 6.17 us  [shards(): lax.psum((grad_all_part[:, :2 * features], grad_all_part[:, 2 * features:...]
    psum x0 -> x1, blocking collectives: none -> 23 us  [shards(): lax.psum(lax.psum((grad_all_part[:, :2 * features], grad_all_part[:, 2 *...]
  transfers between devices with their start and end apart: 9 -> 10, of which waited for: 3 -> 4; matrix products, arithmetic and copies ran while one was open for 9% -> 8% of each run, Pallas kernels for 0% -> 0%
where the time goes in v1:
time: 932 us; the launch traced here: 921 us
  matrix products  323 us (35%)
  waiting for transfers between devices  230 us (25%)
  local copies, waits for them, and re-layouts  215 us (23%)
  other arithmetic  76.7 us (8%)
  blocking collectives  29.2 us (3%)
  starting transfers between devices  23 us (2%)
  between operations  15.4 us (2%)
    psum x1, waiting for transfers between devices, shards(): lax.psum(lax.psum((grad_all_part[:, :2 * features], grad_all_part[:, 2 *...  110 us
    dot_general x4, matrix products, attend_block(): jnp.einsum('hij,ihd->jhd', grad_scores, queries, preferred_element_type=j...  103 us
    psum x1, waiting for transfers between devices, shards(): lax.psum((grad_all_part[:, :2 * features], grad_all_part[:, 2 * features:...  90.1 us
    dot_general x4, matrix products, attend_block(): jnp.einsum('hij,jhd->ihd', grad_scores, key_rows, preferred_element_type=...  76.5 us
    reshape x8, local copies, waits for them, and re-layouts, attend_block(): grad_keys.reshape(slots, row_count, features)  37.3 us
    reshape x8, local copies, waits for them, and re-layouts, attend_block(): grad_values.reshape(slots, row_count, features)  37.3 us
    sub x4, matrix products, attend_block(): powers = jnp.exp(scores - row_max)  33.7 us
    scatter-add x4, other arithmetic, per_block(): key_total = totals[0].at[key_ids].add(key_terms)  33.5 us
  transfers between devices with their start and end apart: 10, of which 4 were waited for; matrix products, arithmetic and copies ran while one was open for 8% of the time, Pallas kernels for 0%

profile of v1, /device:TPU:0, one launch (start us, length us, event | category | flops | bytes accessed | tf_op | source)
XLA Modules:
  0.0 921.1 jit_solution(1047475260448560742)
XLA Ops:
  57.7 15.0 %collective-permute-done = bf16[2,256,1024]{2,0,1:T(2,128)(2,1)} collective-permute-done((bf16[2,256,1024]{2,0,1:T(2,128)(2,1)}, bf16[2,256,1024]{2,0,1:T(2,128)(2,1)}, u32[]{:S(2)}, u32[]{:S(2)}) %collective-permute-start) | collective-permute-done | bytes 1048608 | tf_op jit(solution)/shard_map/ppermute | solution.py:16
  86.7 490.7 %while.16 = (s32[]{:T(128)}, f32[12,256,512]{2,1,0:T(8,128)}, f32[12,256,512]{2,1,0:T(8,128)}, bf16[4,256,512]{2,1,0:T(8,128)(2,1)}, bf16[4,256,512]{2,1,0:T(8,1...) while((s32[]{:T(128)}, f32[12,256,512]{2,1,0:T(8,128)}, ...), condition=%wide.region_18.19_spmd, body=%wide.region_12.18_spmd.sunk | while | flops 2759343360 | bytes 145281360 | solution.py:181
  98.4 8.4 fusion.202
  116.2 19.1 %fusion.204 = bf16[8,64,256]{2,1,0:T(8,128)(2,1)S(1)} fusion(bf16[1280,8,64]{0,2,1:T(8,128)(2,1)} %bitcast.160, f32[8,256,1280]{2,1,0:T(8,128)} %fusion.201, f32[8,256,1280]{2,1,0:T(8,128)} %get-tuple-element.231, f32[8,256]{1,0:T(8,128)S(1)} %get-tuple-element.232), kind=kOutput, calls=%fused_computation.29.clone.1 | convolution fusion | flops 354028800 | bytes 22552576 | tf_op jit(solution)/shard_map/while/body/eval_jaxpr/hij,jhd->ihd/dot_general | solution.py:51
  141.4 25.7 %fusion.203 = f32[1280,8,64]{0,2,1:T(8,128)} fusion(bf16[256,8,64]{0,2,1:T(8,128)(2,1)S(1)} %bitcast.167, f32[8,256,1280]{2,1,0:T(8,128)} %fusion.201, f32[8,256,1280]{2,1,0:T(8,128)} %get-tuple-element.231, f32[8,256]{1,0:T(8,128)S(1)} %get-tuple-element.232), kind=kOutput, calls=%fused_computation.23.clone.1 | convolution fusion | flops 353897728 | bytes 23863296 | tf_op jit(solution)/shard_map/while/body/eval_jaxpr/hij,ihd->jhd/dot_general | solution.py:54
  176.4 8.5 scatter_fusion
  199.2 8.4 scatter_fusion.1
  219.3 8.4 fusion.202
  237.2 19.1 %fusion.204 = bf16[8,64,256]{2,1,0:T(8,128)(2,1)S(1)} fusion(bf16[1280,8,64]{0,2,1:T(8,128)(2,1)} %bitcast.160, f32[8,256,1280]{2,1,0:T(8,128)} %fusion.201, f32[8,256,1280]{2,1,0:T(8,128)} %get-tuple-element.231, f32[8,256]{1,0:T(8,128)S(1)} %get-tuple-element.232), kind=kOutput, calls=%fused_computation.29.clone.1 | convolution fusion | flops 354028800 | bytes 22552576 | tf_op jit(solution)/shard_map/while/body/eval_jaxpr/hij,jhd->ihd/dot_general | solution.py:51
  262.3 25.7 %fusion.203 = f32[1280,8,64]{0,2,1:T(8,128)} fusion(bf16[256,8,64]{0,2,1:T(8,128)(2,1)S(1)} %bitcast.167, f32[8,256,1280]{2,1,0:T(8,128)} %fusion.201, f32[8,256,1280]{2,1,0:T(8,128)} %get-tuple-element.231, f32[8,256]{1,0:T(8,128)S(1)} %get-tuple-element.232), kind=kOutput, calls=%fused_computation.23.clone.1 | convolution fusion | flops 353897728 | bytes 23863296 | tf_op jit(solution)/shard_map/while/body/eval_jaxpr/hij,ihd->jhd/dot_general | solution.py:54
  297.3 8.4 scatter_fusion
  320.1 8.4 scatter_fusion.1
  340.2 8.4 fusion.202
  358.0 19.1 %fusion.204 = bf16[8,64,256]{2,1,0:T(8,128)(2,1)S(1)} fusion(bf16[1280,8,64]{0,2,1:T(8,128)(2,1)} %bitcast.160, f32[8,256,1280]{2,1,0:T(8,128)} %fusion.201, f32[8,256,1280]{2,1,0:T(8,128)} %get-tuple-element.231, f32[8,256]{1,0:T(8,128)S(1)} %get-tuple-element.232), kind=kOutput, calls=%fused_computation.29.clone.1 | convolution fusion | flops 354028800 | bytes 22552576 | tf_op jit(solution)/shard_map/while/body/eval_jaxpr/hij,jhd->ihd/dot_general | solution.py:51
  383.1 25.7 %fusion.203 = f32[1280,8,64]{0,2,1:T(8,128)} fusion(bf16[256,8,64]{0,2,1:T(8,128)(2,1)S(1)} %bitcast.167, f32[8,256,1280]{2,1,0:T(8,128)} %fusion.201, f32[8,256,1280]{2,1,0:T(8,128)} %get-tuple-element.231, f32[8,256]{1,0:T(8,128)S(1)} %get-tuple-element.232), kind=kOutput, calls=%fused_computation.23.clone.1 | convolution fusion | flops 353897728 | bytes 23863296 | tf_op jit(solution)/shard_map/while/body/eval_jaxpr/hij,ihd->jhd/dot_general | solution.py:54
  418.2 8.4 scatter_fusion
  440.9 8.3 scatter_fusion.1
  461.0 8.4 fusion.202
  478.8 19.1 %fusion.204 = bf16[8,64,256]{2,1,0:T(8,128)(2,1)S(1)} fusion(bf16[1280,8,64]{0,2,1:T(8,128)(2,1)} %bitcast.160, f32[8,256,1280]{2,1,0:T(8,128)} %fusion.201, f32[8,256,1280]{2,1,0:T(8,128)} %get-tuple-element.231, f32[8,256]{1,0:T(8,128)S(1)} %get-tuple-element.232), kind=kOutput, calls=%fused_computation.29.clone.1 | convolution fusion | flops 354028800 | bytes 22552576 | tf_op jit(solution)/shard_map/while/body/eval_jaxpr/hij,jhd->ihd/dot_general | solution.py:51
  503.9 25.7 %fusion.203 = f32[1280,8,64]{0,2,1:T(8,128)} fusion(bf16[256,8,64]{0,2,1:T(8,128)(2,1)S(1)} %bitcast.167, f32[8,256,1280]{2,1,0:T(8,128)} %fusion.201, f32[8,256,1280]{2,1,0:T(8,128)} %get-tuple-element.231, f32[8,256]{1,0:T(8,128)S(1)} %get-tuple-element.232), kind=kOutput, calls=%fused_computation.23.clone.1 | convolution fusion | flops 353897728 | bytes 23863296 | tf_op jit(solution)/shard_map/while/body/eval_jaxpr/hij,ihd->jhd/dot_general | solution.py:54
  626.8 15.0 %collective-permute-done.5 = bf16[2,256,1024]{2,0,1:T(2,128)(2,1)} collective-permute-done((bf16[2,256,1024]{2,0,1:T(2,128)(2,1)S(1)}, bf16[2,256,1024]{2,0,1:T(2,128)(2,1)}, u32[]{:S(2)}, u32[]{:S(2)}) %collective-permute-start.5) | collective-permute-done | bytes 1048608 | tf_op jit(solution)/shard_map/ppermute | solution.py:16
  657.7 90.1 %all-reduce.8.cloned.1.call-done = (f32[512,1024]{1,0:T(8,128)}, f32[512,512]{1,0:T(8,128)}, f32[512,512]{1,0:T(8,128)}) async-done(((f32[512,1024]{1,0:T(8,128)}, f32[512,512]{1,0:T(8,128)}, f32[512,512]{1,0:T(8,128)}), (f32[512,1024]{1,0:T(8,128)}, f32[512,512]{1,0:T(8,128)}, f32[512,512]{1,0:T(8,128)})) %all-reduce.8.cloned.1.call-update) | async-done | bytes 4194320 | tf_op jit(solution)/shard_map/psum | solution.py:228
  775.2 23.0 %psum.63 = f32[512]{0:T(512)} all-reduce(f32[512]{0:T(512)S(1)} %psum.62), channel_id=1, replica_groups=mesh['bx'=8,'by'=4] {'bx'}, use_global_device_ids=true, to_apply=%region_29.30 | all-reduce | flops 512 | bytes 4096 | tf_op jit(solution)/shard_map/psum | solution.py:227
  798.2 110.4 %all-reduce.6.cloned.1.call-done = (f32[512,1024]{1,0:T(8,128)}, f32[512,512]{1,0:T(8,128)}, f32[512,512]{1,0:T(8,128)}) async-done(((f32[512,1024]{1,0:T(8,128)}, f32[512,512]{1,0:T(8,128)}, f32[512,512]{1,0:T(8,128)}), (f32[512,1024]{1,0:T(8,128)}, f32[512,512]{1,0:T(8,128)}, f32[512,512]{1,0:T(8,128)})) %all-reduce.6.cloned.1.call-update) | async-done | bytes 4194320 | tf_op jit(solution)/shard_map/psum | solution.py:227
  (315 shorter events, 380.6 us)
Async XLA Ops:
  7.2 740.6 %all-reduce.8.cloned.1.call-start = ((), (), s32[]{:S(2)}) async-start(), calls=%async_computation.1 | async-start | bytes 8388608 | tf_op jit(solution)/shard_map/psum | solution.py:228
  15.4 38.5 %copy-start.6 = (bf16[1024,512]{1,0:T(8,128)(2,1)}, bf16[1024,512]{1,0:T(8,128)(2,1)S(1)}, u32[]{:S(2)}) copy-start(bf16[1024,512]{1,0:T(8,128)(2,1)S(1)} %gather_fusion.1) | copy-start | bytes 3145732
  16.3 37.6 %copy-start.20 = (f32[1024]{0:T(1024)}, f32[1024]{0:T(1024)S(1)}, u32[]{:S(2)}) copy-start(f32[1024]{0:T(1024)S(1)} %get-tuple-element.148) | copy-start | bytes 12292
  22.6 50.0 %collective-permute-start = (bf16[2,256,1024]{2,0,1:T(2,128)(2,1)}, bf16[2,256,1024]{2,0,1:T(2,128)(2,1)}, u32[]{:S(2)}, u32[]{:S(2)}) collective-permute-start(bf16[2,256,1024]{2,0,1:T(2,128)(2,1)} %convolution_convert_fusion.4), channel_id=1, source_target_pairs={{0,4},{4,8},{8,12},{12,16},{16,20},{20,24},{24,28},{1,5},{5,9},{9,... | collective-permute-start | bytes 3145736 | tf_op jit(solution)/shard_map/ppermute | solution.py:16
  33.1 41.0 %collective-permute-start.1 = (bf16[2,256,1024]{2,0,1:T(2,128)(2,1)}, bf16[2,256,1024]{2,0,1:T(2,128)(2,1)}, u32[]{:S(2)}, u32[]{:S(2)}) collective-permute-start(bf16[2,256,1024]{2,0,1:T(2,128)(2,1)} %convolution_convert_fusion.3), channel_id=1, source_target_pairs={{4,0},{8,4},{12,8},{16,12},{20,16},{24,20},{28,24},{5,1},{9,5},{13... | collective-permute-start | bytes 3145736 | tf_op jit(solution)/shard_map/ppermute | solution.py:16
  34.6 11.6 %copy-start.30 = (pred[4]{0:T(512)(128)(4,1)}, pred[4]{0:T(512)(128)(4,1)S(1)}, u32[]{:S(2)}) copy-start(pred[4]{0:T(512)(128)(4,1)S(1)} %fusion.69) | copy-start | bytes 16
  39.1 36.5 %collective-permute-start.2 = (bf16[2,256,1024]{2,0,1:T(2,128)(2,1)}, bf16[2,256,1024]{2,0,1:T(2,128)(2,1)}, u32[]{:S(2)}, u32[]{:S(2)}) collective-permute-start(bf16[2,256,1024]{2,0,1:T(2,128)(2,1)} %convolution_convert_fusion.2), channel_id=1, source_target_pairs={{0,1},{1,2},{2,3},{4,5},{5,6},{6,7},{8,9},{9,10},{10,11},{12,13},{... | collective-permute-start | bytes 3145736 | tf_op jit(solution)/shard_map/ppermute | solution.py:16
  46.2 30.9 %collective-permute-start.3 = (bf16[2,256,1024]{2,0,1:T(2,128)(2,1)}, bf16[2,256,1024]{2,0,1:T(2,128)(2,1)}, u32[]{:S(2)}, u32[]{:S(2)}) collective-permute-start(bf16[2,256,1024]{2,0,1:T(2,128)(2,1)} %convolution_convert_fusion.1), channel_id=1, source_target_pairs={{1,0},{2,1},{3,2},{5,4},{6,5},{7,6},{9,8},{10,9},{11,10},{13,12},{... | collective-permute-start | bytes 3145736 | tf_op jit(solution)/shard_map/ppermute | solution.py:16
  116.2 19.3 %copy-start.2 = (bf16[1280,512]{0,1:T(8,128)(2,1)S(1)}, bf16[1280,512]{0,1:T(8,128)(2,1)}, u32[]{:S(2)}) copy-start(bf16[1280,512]{0,1:T(8,128)(2,1)} %copy.109) | copy-start | bytes 3932164 | tf_op jit(solution)/shard_map/while
  237.2 19.3 %copy-start.2 = (bf16[1280,512]{0,1:T(8,128)(2,1)S(1)}, bf16[1280,512]{0,1:T(8,128)(2,1)}, u32[]{:S(2)}) copy-start(bf16[1280,512]{0,1:T(8,128)(2,1)} %copy.109) | copy-start | bytes 3932164 | tf_op jit(solution)/shard_map/while
  358.0 19.3 %copy-start.2 = (bf16[1280,512]{0,1:T(8,128)(2,1)S(1)}, bf16[1280,512]{0,1:T(8,128)(2,1)}, u32[]{:S(2)}) copy-start(bf16[1280,512]{0,1:T(8,128)(2,1)} %copy.109) | copy-start | bytes 3932164 | tf_op jit(solution)/shard_map/while
  478.8 19.3 %copy-start.2 = (bf16[1280,512]{0,1:T(8,128)(2,1)S(1)}, bf16[1280,512]{0,1:T(8,128)(2,1)}, u32[]{:S(2)}) copy-start(bf16[1280,512]{0,1:T(8,128)(2,1)} %copy.109) | copy-start | bytes 3932164 | tf_op jit(solution)/shard_map/while
  585.5 19.3 %slice-start = ((s8[6291456]{0:T(1024)(128)(4,1)}), s8[4194304]{0:T(1024)(128)(4,1)S(1)}, s32[]{:S(2)}) async-start(s8[6291456]{0:T(1024)(128)(4,1)} %bitcast.152), calls=%async_computation.2 | async-start | bytes 8388608
  588.9 15.9 %slice-start.1 = ((s8[6291456]{0:T(1024)(128)(4,1)}), s8[2097152]{0:T(1024)(128)(4,1)S(1)}, s32[]{:S(2)}) async-start(s8[6291456]{0:T(1024)(128)(4,1)} %bitcast.152), calls=%async_computation.3 | async-start | bytes 4194304
  592.6 31.4 %collective-permute-start.4 = (bf16[2,256,1024]{2,0,1:T(2,128)(2,1)}, bf16[2,256,1024]{2,0,1:T(2,128)(2,1)}, u32[]{:S(2)}, u32[]{:S(2)}) collective-permute-start(bf16[2,256,1024]{2,0,1:T(2,128)(2,1)} %pad_maximum_fusion.3), channel_id=1, source_target_pairs={{4,0},{8,4},{12,8},{16,12},{20,16},{24,20},{28,24},{5,1},{9,5},{13... | collective-permute-start | bytes 3145736 | tf_op jit(solution)/shard_map/ppermute | solution.py:16
  594.8 47.1 %collective-permute-start.5 = (bf16[2,256,1024]{2,0,1:T(2,128)(2,1)S(1)}, bf16[2,256,1024]{2,0,1:T(2,128)(2,1)}, u32[]{:S(2)}, u32[]{:S(2)}) collective-permute-start(bf16[2,256,1024]{2,0,1:T(2,128)(2,1)S(1)} %pad_maximum_fusion.4), channel_id=1, source_target_pairs={{0,4},{4,8},{8,12},{12,16},{16,20},{20,24},{24,28},{1,5},{5,9},{9,... | collective-permute-start | bytes 3145736 | tf_op jit(solution)/shard_map/ppermute | solution.py:16
  601.5 43.1 %collective-permute-start.6 = (bf16[2,256,1024]{2,0,1:T(2,128)(2,1)S(1)}, bf16[2,256,1024]{2,0,1:T(2,128)(2,1)}, u32[]{:S(2)}, u32[]{:S(2)}) collective-permute-start(bf16[2,256,1024]{2,0,1:T(2,128)(2,1)S(1)} %pad_maximum_fusion.5), channel_id=1, source_target_pairs={{1,0},{2,1},{3,2},{5,4},{6,5},{7,6},{9,8},{10,9},{11,10},{13,12},{... | collective-permute-start | bytes 3145736 | tf_op jit(solution)/shard_map/ppermute | solution.py:16
  615.5 32.0 %collective-permute-start.7 = (bf16[2,256,1024]{2,0,1:T(2,128)(2,1)}, bf16[2,256,1024]{2,0,1:T(2,128)(2,1)S(1)}, u32[]{:S(2)}, u32[]{:S(2)}) collective-permute-start(bf16[2,256,1024]{2,0,1:T(2,128)(2,1)} %pad_maximum_fusion.6), channel_id=1, source_target_pairs={{0,1},{1,2},{2,3},{4,5},{5,6},{6,7},{8,9},{9,10},{10,11},{12,13},{... | collective-permute-start | bytes 3145736 | tf_op jit(solution)/shard_map/ppermute | solution.py:16
  623.9 17.9 %copy-start.29 = (pred[4]{0:T(512)(128)(4,1)S(1)}, pred[4]{0:T(512)(128)(4,1)}, u32[]{:S(2)}) copy-start(pred[4]{0:T(512)(128)(4,1)} %copy-done.28) | copy-start | bytes 16
  623.9 17.9 %copy-start.37 = (s32[4]{0:T(128)S(1)}, s32[4]{0:T(128)}, u32[]{:S(2)}) copy-start(s32[4]{0:T(128)} %copy-done.36) | copy-start | bytes 52
  626.8 17.9 %copy-start.31 = (pred[4]{0:T(512)(128)(4,1)S(1)}, pred[4]{0:T(512)(128)(4,1)}, u32[]{:S(2)}) copy-start(pred[4]{0:T(512)(128)(4,1)} %copy-done.30) | copy-start | bytes 16
  626.8 17.9 %copy-start.39 = (s32[4]{0:T(128)S(1)}, s32[4]{0:T(128)}, u32[]{:S(2)}) copy-start(s32[4]{0:T(128)} %copy-done.38) | copy-start | bytes 52
  657.7 94.9 %copy-start.41 = (bf16[4,256,512]{2,1,0:T(8,128)(2,1)S(1)}, bf16[4,256,512]{2,1,0:T(8,128)(2,1)}, u32[]{:S(2)}) copy-start(bf16[4,256,512]{2,1,0:T(8,128)(2,1)} %get-tuple-element.61) | copy-start | bytes 3145732
  657.7 250.9 %all-reduce.6.cloned.1.call-start = ((), (), s32[]{:S(2)}) async-start(), calls=%async_computation | async-start | bytes 8388608 | tf_op jit(solution)/shard_map/psum | solution.py:227
  (41 other events, 196.1 us)
Sparse Core Ops, SparseCore 0:
  657.8 89.9 all-reduce.7
  751.7 156.7 all-reduce.5
